TPU v7x, 32 devices: a whole 2x2x4 slice. The times are simulated.
32 devices in a mesh: blk: 8 (over y, x, core), chan: 4 (over z).
Axes of the slice: x: 2, y: 2, z: 4, core: 2. Of those that a mesh axis runs over, the one named last changes fastest.
Arguments:
- positions: float32 [3, 1024], P(None, 'blk'), may hold values from 0 to 48, as said below
- species: int32 [1024], P('blk'), may hold values from 0 to 1
- node_features: float32 [64, 1024], P('chan', 'blk'), may hold values from -6 to 6
- block_mask: int32 [8, 7], P('blk'), may hold values from 0 to 1, as said below
- radial_weight: float32 [8, 64], P(None, 'chan'), may hold values from -2 to 2
- species_embed: float32 [64, 2], P('chan'), may hold values from 0.25 to 1.75
- center_embed: float32 [64, 2], P('chan'), may hold values from 0.25 to 1.75
- mix_weight: float32 [3, 64, 64], replicated, may hold values from -0.75 to 0.75
Outputs:
- descriptors: float32 [3, 64, 1024], P(None, 'chan', 'blk')
Inputs may be any that keep to these rules, and one draw needn't show every extreme that they name: `positions`: atom g lies in slab s = g // 128: its first coordinate in [s * 5 / 3, (s + 1) * 5 / 3), the other two in [0, 48). An arbitrary set of kept slab pairs, symmetric between the two slabs of a pair: block_mask[i, 3 + k] equals block_mask[(i + k) mod 8, 3 - k]; the middle column is 1.
All inputs are finite; a program needn't handle non-finite values.
Results may differ from a plain program's by a relative error of at most 0.0035.
Values sent between devices are 32-bit elements; how exact they have to be, the bound alone decides.
No kernel may reach another device: no remote copies, remote signals or barrier semaphores. Data moves between devices by JAX's collectives and lax.ppermute only.
A program may use at most 64 MiB of HBM per device.

v0:
```python
import math
import jax
import jax.numpy as jnp
from jax import lax
from jax.sharding import PartitionSpec as P

slab_width = 5.0 / 3.0
cross_width = 48.0
cut_radius = 5.0
soften = 0.25


def from_behind(value, axis, by):
    size = lax.axis_size(axis)
    return lax.ppermute(value, axis, [(i, (i + by) % size) for i in range(size)])


def table_of(own_pos, other_pos, box_x, keep_pairs, count):
    separation = other_pos[:, None, :] - own_pos[:, :, None]
    lengths = jnp.array([box_x, cross_width, cross_width], dtype=jnp.float32)[:, None, None]
    separation = separation - lengths * jnp.floor(separation / lengths + 0.5)
    distance = jnp.sqrt(jnp.sum(separation * separation, axis=0) + soften)
    unit_x = separation[0] / distance
    unit_y = separation[1] / distance
    unit_z = separation[2] / distance
    root3 = math.sqrt(3.0)
    root15 = math.sqrt(15.0)
    harmonics = jnp.stack(
        [
            jnp.ones_like(distance),
            root3 * unit_x,
            root3 * unit_y,
            root3 * unit_z,
            root15 * unit_x * unit_y,
            root15 * unit_y * unit_z,
            0.5 * math.sqrt(5.0) * (2.0 * unit_z * unit_z - unit_x * unit_x - unit_y * unit_y),
            root15 * unit_x * unit_z,
            0.5 * root15 * (unit_x * unit_x - unit_y * unit_y),
        ]
    )
    scaled = distance / cut_radius
    polynomial = 1.0 - 28.0 * scaled**6 + 48.0 * scaled**7 - 21.0 * scaled**8
    envelope = jnp.where(scaled < 1.0, polynomial, 0.0) * keep_pairs
    orders = jnp.arange(1, count + 1, dtype=jnp.float32)[:, None, None]
    radial = (
        math.sqrt(2.0 / cut_radius)
        * jnp.sin(orders * (math.pi / cut_radius) * distance[None])
        / distance[None]
        * envelope[None]
    )
    return (radial[:, None] * harmonics[None]).astype(jnp.bfloat16)


def weights_lm(mix_weight):
    return jnp.concatenate(
        [
            mix_weight[0:1],
            jnp.repeat(mix_weight[1:2], 3, axis=0),
            jnp.repeat(mix_weight[2:3], 5, axis=0),
        ],
        axis=0,
    )


def describe(mixed_tensor):
    squares = mixed_tensor * mixed_tensor
    return jnp.log1p(
        jnp.stack(
            [squares[:, 0], jnp.sum(squares[:, 1:4], axis=1), jnp.sum(squares[:, 4:9], axis=1)]
        )
    )


def one_hot_of(species, kinds):
    return (species[None, :] == jnp.arange(kinds, dtype=jnp.int32)[:, None]).astype(jnp.float32)


def carried_of(species, node_features, species_embed, radial_weight):
    embedded = jnp.dot(
        species_embed, one_hot_of(species, species_embed.shape[1]), precision=lax.Precision.HIGHEST
    )
    return (radial_weight[:, :, None] * (node_features * embedded)[None]).astype(jnp.bfloat16)


def contributions(own_pos, other_pos, other_carried, active, box_x, count):
    forward_shape = (other_carried.shape[1], 9, own_pos.shape[1])

    def compute():
        pair_table = table_of(own_pos, other_pos, box_x, active.astype(jnp.float32), count)
        forward = jnp.einsum(
            "ncb,nmab->cma", other_carried, pair_table, preferred_element_type=jnp.float32
        )
        return forward

    def skipped():
        return jnp.zeros(forward_shape, jnp.float32)

    return lax.cond(active > 0, compute, skipped)


def step_ahead(bundle):
    return from_behind(bundle, "blk", -1)


def shards(
    positions,
    species,
    node_features,
    block_mask,
    radial_weight,
    species_embed,
    center_embed,
    mix_weight,
):
    box_x = float(lax.axis_size("blk")) * slab_width
    reach = (block_mask.shape[1] - 1) // 2
    count = radial_weight.shape[0]
    atom_count = positions.shape[1]
    feats_all, spec_all, cent_all, radial_all = (
        node_features,
        species_embed,
        center_embed,
        radial_weight,
    )
    centre_rows = jnp.arange(atom_count, dtype=jnp.int32)
    no_self = 1.0 - (
        centre_rows[:, None] == jnp.arange(atom_count, dtype=jnp.int32)[None, :]
    ).astype(jnp.float32)
    slab_carried = carried_of(species, feats_all, spec_all, radial_all)
    self_table = table_of(
        positions, positions, box_x, block_mask[0, reach].astype(jnp.float32) * no_self, count
    )
    summed = jnp.einsum(
        "ncb,nmab->cma", slab_carried, self_table, preferred_element_type=jnp.float32
    )
    ahead = (positions, species, feats_all)
    behind = ahead
    for offset in range(1, reach + 1):
        ahead = step_ahead(ahead)
        ahead_carried = carried_of(ahead[1], ahead[2], spec_all, radial_all)
        summed = summed + contributions(
            positions, ahead[0], ahead_carried, block_mask[0, reach + offset], box_x, count
        )
        behind = from_behind((behind[0], behind[1], behind[2]), "blk", 1)
        behind_carried = carried_of(behind[1], behind[2], spec_all, radial_all)
        summed = summed + contributions(
            positions, behind[0], behind_carried, block_mask[0, reach - offset], box_x, count
        )
    centre = jnp.dot(
        cent_all, one_hot_of(species, cent_all.shape[1]), precision=lax.Precision.HIGHEST
    )
    features = summed * centre[:, None, :]
    weights_all = weights_lm(mix_weight)
    channel_count = features.shape[0]
    weights_out = lax.dynamic_slice_in_dim(
        weights_all, lax.axis_index("chan") * channel_count, channel_count, 1
    )
    mixed_tensor = jnp.einsum(
        "mpc,cma->pma",
        weights_out,
        lax.all_gather(features, "chan", axis=0, tiled=True),
        precision=lax.Precision.HIGHEST,
    )
    return describe(mixed_tensor)


def solution(mesh):
    return jax.shard_map(
        shards,
        mesh=mesh,
        in_specs=(
            P(None, "blk"),
            P("blk"),
            P("chan", "blk"),
            P("blk", None),
            P(None, "chan"),
            P("chan", None),
            P("chan", None),
            P(),
        ),
        out_specs=P(None, "chan", "blk"),
        check_vma=False,
    )
```

profile of v0, /device:TPU:0, one launch (start us, length us, event | category | flops | bytes accessed | tf_op | source)
XLA Modules:
  0.0 70.0 jit_solution(16418820313768697507)
XLA Ops:
  0.5 2.9 %collective-permute-start.2 = (s32[128]{0:T(128)}, s32[128]{0:T(128)S(1)}, u32[]{:S(2)}, u32[]{:S(2)}) collective-permute-start(s32[128]{0:T(128)} %param.28), channel_id=1, source_target_pairs={{0,28},{4,0},{8,4},{12,8},{16,12},{20,16},{24,20},{28,24},{1,29},{... | collective-permute-start | bytes 1544 | tf_op jit(solution)/shard_map/ppermute | solution.py:15
  4.9 0.9 %multiply_reduce_fusion.6 = (f32[128,128]{1,0:T(8,128)S(1)}, f32[3,128,128]{2,1,0:T(8,128)S(1)}) fusion(f32[3]{0:T(128)} %constant.184, f32[3]{0:T(128)} %constant.182.clone, f32[3,128]{1,0:T(4,128)} %param.27), kind=kLoop, calls=%fused_computation.331 | loop fusion | flops 376832 | bytes 263704 | tf_op jit(solution)/shard_map/reduce_sum | solution.py:22
  8.5 1.8 %divide_multiply_fusion.6 = f32[8,128,128]{2,1,0:T(8,128)S(1)} fusion(f32[128,128]{1,0:T(8,128)S(1)} %get-tuple-element.162, f32[128,128]{1,0:T(8,128)S(1)} %get-tuple-element.161, f32[8]{0:T(128)S(1)} %add_multiply_fusion.7), kind=kLoop, calls=%fused_computation.322 | loop fusion | flops 524288 | bytes 655392 | tf_op jit(solution)/shard_map/mul | solution.py:46
  13.0 1.9 %collective-permute-start.6 = (f32[3,128]{1,0:T(4,128)S(1)}, f32[3,128]{1,0:T(4,128)S(1)}, u32[]{:S(2)}, u32[]{:S(2)}) collective-permute-start(f32[3,128]{1,0:T(4,128)S(1)} %collective-permute-done), channel_id=1, source_target_pairs={{0,28},{4,0},{8,4},{12,8},{16,12},{20,16},{24,20},{28,24},{1,29},{... | collective-permute-start | bytes 4616 | tf_op jit(solution)/shard_map/ppermute | solution.py:15
  17.6 2.0 %collective-permute-start.8 = (s32[128]{0:T(128)S(1)}, s32[128]{0:T(128)S(1)}, u32[]{:S(2)}, u32[]{:S(2)}) collective-permute-start(s32[128]{0:T(128)S(1)} %collective-permute-done.2), channel_id=1, source_target_pairs={{0,28},{4,0},{8,4},{12,8},{16,12},{20,16},{24,20},{28,24},{1,29},{... | collective-permute-start | bytes 1544 | tf_op jit(solution)/shard_map/ppermute | solution.py:15
  19.6 1.2 %collective-permute-done.11 = s32[128]{0:T(128)S(1)} collective-permute-done((s32[128]{0:T(128)S(1)}, s32[128]{0:T(128)S(1)}, u32[]{:S(2)}, u32[]{:S(2)}) %collective-permute-start.11) | collective-permute-done | bytes 544 | tf_op jit(solution)/shard_map/ppermute | solution.py:15
  20.9 1.0 %collective-permute-start.17 = (s32[128]{0:T(128)S(1)}, s32[128]{0:T(128)S(1)}, u32[]{:S(2)}, u32[]{:S(2)}) collective-permute-start(s32[128]{0:T(128)S(1)} %collective-permute-done.11), channel_id=1, source_target_pairs={{0,4},{4,8},{8,12},{12,16},{16,20},{20,24},{24,28},{28,0},{1,5},{5... | collective-permute-start | bytes 1544 | tf_op jit(solution)/shard_map/ppermute | solution.py:15
  21.9 1.7 %collective-permute-start.14 = (s32[128]{0:T(128)S(1)}, s32[128]{0:T(128)S(1)}, u32[]{:S(2)}, u32[]{:S(2)}) collective-permute-start(s32[128]{0:T(128)S(1)} %collective-permute-done.8), channel_id=1, source_target_pairs={{0,28},{4,0},{8,4},{12,8},{16,12},{20,16},{24,20},{28,24},{1,29},{... | collective-permute-start | bytes 1544 | tf_op jit(solution)/shard_map/ppermute | solution.py:15
  25.1 3.1 %collective-permute-done.10 = f32[16,128]{1,0:T(8,128)S(1)} collective-permute-done((f32[16,128]{1,0:T(8,128)S(1)}, f32[16,128]{1,0:T(8,128)S(1)}, u32[]{:S(2)}, u32[]{:S(2)}) %collective-permute-start.10) | collective-permute-done | bytes 8224 | tf_op jit(solution)/shard_map/ppermute | solution.py:15
  28.4 1.2 %collective-permute-done.7 = f32[16,128]{1,0:T(8,128)S(1)} collective-permute-done((f32[16,128]{1,0:T(8,128)S(1)}, f32[16,128]{1,0:T(8,128)S(1)}, u32[]{:S(2)}, u32[]{:S(2)}) %collective-permute-start.7) | collective-permute-done | bytes 8224 | tf_op jit(solution)/shard_map/ppermute | solution.py:15
  30.3 2.2 %collective-permute-start.13 = (f32[16,128]{1,0:T(8,128)S(1)}, f32[16,128]{1,0:T(8,128)S(1)}, u32[]{:S(2)}, u32[]{:S(2)}) collective-permute-start(f32[16,128]{1,0:T(8,128)S(1)} %collective-permute-done.7), channel_id=1, source_target_pairs={{0,28},{4,0},{8,4},{12,8},{16,12},{20,16},{24,20},{28,24},{1,29},{... | collective-permute-start | bytes 24584 | tf_op jit(solution)/shard_map/ppermute | solution.py:15
  32.5 1.1 %collective-permute-done.16 = f32[16,128]{1,0:T(8,128)S(1)} collective-permute-done((f32[16,128]{1,0:T(8,128)S(1)}, f32[16,128]{1,0:T(8,128)S(1)}, u32[]{:S(2)}, u32[]{:S(2)}) %collective-permute-start.16) | collective-permute-done | bytes 8224 | tf_op jit(solution)/shard_map/ppermute | solution.py:15
  34.2 3.7 %conditional.8 = (f32[16,9,128]{2,0,1:T(8,128)S(1)}) conditional(s32[]{:T(128)} %convert_element_type.108, () %tuple.45, (f32[3,128]{1,0:T(4,128)S(1)}, f32[3,128]{1,0:T(4,128)S(1)}, f32[3]{0:T(128)S(1)}, s32[]{:T(128)}, bf16[8,16,128]{2,1,0:T(8,128)(2,1)S(1)}) %tuple.113), branch_computations={%region_7.8_spmd, %region_8.10_spmd} | conditional | flops 41861136 | bytes 4435040 | solution.py:98
  35.4 1.8 %divide_multiply_fusion.2 = f32[8,128,128]{2,1,0:T(8,128)S(1)} fusion(f32[128,128]{1,0:T(8,128)S(1)} %get-tuple-element.143, f32[128,128]{1,0:T(8,128)S(1)} %get-tuple-element.142, f32[8]{0:T(128)S(1)} %add_multiply_fusion.2), kind=kLoop, calls=%fused_computation.105 | loop fusion | flops 524288 | bytes 655392 | tf_op jit(solution)/shard_map/cond/branch_1_fun/mul | solution.py:46
  37.9 4.5 %conditional.9 = (f32[16,9,128]{2,0,1:T(8,128)S(1)}) conditional(s32[]{:T(128)} %convert_element_type.110, () %tuple.47, (f32[3,128]{1,0:T(4,128)}, f32[3,128]{1,0:T(4,128)S(1)}, f32[3]{0:T(128)S(1)}, s32[]{:T(128)}, bf16[8,16,128]{2,1,0:T(8,128)(2,1)S(1)}) %tuple.114), branch_computations={%region_10.11_spmd, %region_11.13_spmd} | conditional | flops 41861136 | bytes 4435040 | solution.py:98
  38.0 0.8 %multiply_reduce_fusion.3 = (f32[128,128]{1,0:T(8,128)S(1)}, f32[3,128,128]{2,1,0:T(8,128)S(1)}) fusion(f32[3]{0:T(128)S(1)} %get-tuple-element.100, f32[3,128]{1,0:T(4,128)S(1)} %get-tuple-element.99, f32[3,128]{1,0:T(4,128)} %get-tuple-element.98), kind=kLoop, calls=%fused_computation.161 | loop fusion | flops 376832 | bytes 265228 | tf_op jit(solution)/shard_map/cond/branch_1_fun/reduce_sum | solution.py:22
  39.9 1.8 %divide_multiply_fusion.3 = f32[8,128,128]{2,1,0:T(8,128)S(1)} fusion(f32[128,128]{1,0:T(8,128)S(1)} %get-tuple-element.147, f32[128,128]{1,0:T(8,128)S(1)} %get-tuple-element.146, f32[8]{0:T(128)S(1)} %add_multiply_fusion.3), kind=kLoop, calls=%fused_computation.155 | loop fusion | flops 524288 | bytes 655392 | tf_op jit(solution)/shard_map/cond/branch_1_fun/mul | solution.py:46
  42.4 3.7 %conditional.11 = (f32[16,9,128]{2,0,1:T(8,128)S(1)}) conditional(s32[]{:T(128)} %convert_element_type.114, () %tuple.51, (f32[3,128]{1,0:T(4,128)S(1)}, f32[3,128]{1,0:T(4,128)S(1)}, f32[3]{0:T(128)S(1)}, s32[]{:T(128)}, bf16[8,16,128]{2,1,0:T(8,128)(2,1)S(1)}) %tuple.115), branch_computations={%region_16.17_spmd, %region_17.19_spmd} | conditional | flops 41861136 | bytes 4435040 | solution.py:98
  43.5 1.8 %divide_multiply_fusion.5 = f32[8,128,128]{2,1,0:T(8,128)S(1)} fusion(f32[128,128]{1,0:T(8,128)S(1)} %get-tuple-element.155, f32[128,128]{1,0:T(8,128)S(1)} %get-tuple-element.154, f32[8]{0:T(128)S(1)} %add_multiply_fusion.5), kind=kLoop, calls=%fused_computation.255 | loop fusion | flops 524288 | bytes 655392 | tf_op jit(solution)/shard_map/cond/branch_1_fun/mul | solution.py:46
  46.1 3.7 %conditional.6 = (f32[16,9,128]{2,0,1:T(8,128)S(1)}) conditional(s32[]{:T(128)} %convert_element_type.104, () %tuple.41, (f32[3,128]{1,0:T(4,128)S(1)}, f32[3,128]{1,0:T(4,128)S(1)}, f32[3]{0:T(128)S(1)}, s32[]{:T(128)}, bf16[8,16,128]{2,1,0:T(8,128)(2,1)S(1)}) %tuple.116), branch_computations={%region_1.2_spmd, %region_2.4_spmd} | conditional | flops 41861136 | bytes 4435040 | solution.py:98
  47.3 1.8 %divide_multiply_fusion = f32[8,128,128]{2,1,0:T(8,128)S(1)} fusion(f32[128,128]{1,0:T(8,128)S(1)} %get-tuple-element.135, f32[128,128]{1,0:T(8,128)S(1)} %get-tuple-element.134, f32[8]{0:T(128)S(1)} %add_multiply_fusion), kind=kLoop, calls=%fused_computation.5 | loop fusion | flops 524288 | bytes 655392 | tf_op jit(solution)/shard_map/cond/branch_1_fun/mul | solution.py:46
  49.8 3.8 %conditional.7 = (f32[16,9,128]{2,0,1:T(8,128)S(1)}) conditional(s32[]{:T(128)} %convert_element_type.106, () %tuple.43, (f32[3,128]{1,0:T(4,128)S(1)}, f32[3,128]{1,0:T(4,128)S(1)}, f32[3]{0:T(128)S(1)}, s32[]{:T(128)}, bf16[8,16,128]{2,1,0:T(8,128)(2,1)S(1)}) %tuple.117), branch_computations={%region_4.5_spmd, %region_5.7_spmd} | conditional | flops 41861136 | bytes 4435040 | solution.py:98
  51.0 1.8 %divide_multiply_fusion.1 = f32[8,128,128]{2,1,0:T(8,128)S(1)} fusion(f32[128,128]{1,0:T(8,128)S(1)} %get-tuple-element.139, f32[128,128]{1,0:T(8,128)S(1)} %get-tuple-element.138, f32[8]{0:T(128)S(1)} %add_multiply_fusion.1), kind=kLoop, calls=%fused_computation.55 | loop fusion | flops 524288 | bytes 655392 | tf_op jit(solution)/shard_map/cond/branch_1_fun/mul | solution.py:46
  53.6 15.3 %all_gather.3 = f32[64,9,128]{2,0,1:T(8,128)S(1)} all-gather(f32[16,9,128]{2,0,1:T(8,128)S(1)} %add_multiply_fusion.6), channel_id=1, replica_groups=mesh['blk'=8,'chan'=4] {'chan'}, dimensions={0}, use_global_device_ids=true | all-gather | bytes 368640 | tf_op jit(solution)/shard_map/all_gather | solution.py:161
  (141 shorter events, 15.4 us)
Async XLA Ops:
  0.0 8.0 %copy-start = (f32[16,2]{0,1:T(2,128)S(1)}, f32[16,2]{0,1:T(2,128)}, u32[]{:S(2)}) copy-start(f32[16,2]{0,1:T(2,128)} %param.32) | copy-start | bytes 388
  0.0 16.8 %collective-permute-start.5 = (s32[128]{0:T(128)}, s32[128]{0:T(128)S(1)}, u32[]{:S(2)}, u32[]{:S(2)}) collective-permute-start(s32[128]{0:T(128)} %param.28), channel_id=1, source_target_pairs={{0,4},{4,8},{8,12},{12,16},{16,20},{20,24},{24,28},{28,0},{1,5},{5... | collective-permute-start | bytes 1544 | tf_op jit(solution)/shard_map/ppermute | solution.py:15
  0.5 17.1 %collective-permute-start.2 = (s32[128]{0:T(128)}, s32[128]{0:T(128)S(1)}, u32[]{:S(2)}, u32[]{:S(2)}) collective-permute-start(s32[128]{0:T(128)} %param.28), channel_id=1, source_target_pairs={{0,28},{4,0},{8,4},{12,8},{16,12},{20,16},{24,20},{28,24},{1,29},{... | collective-permute-start | bytes 1544 | tf_op jit(solution)/shard_map/ppermute | solution.py:15
  3.4 9.5 %collective-permute-start = (f32[3,128]{1,0:T(4,128)}, f32[3,128]{1,0:T(4,128)S(1)}, u32[]{:S(2)}, u32[]{:S(2)}) collective-permute-start(f32[3,128]{1,0:T(4,128)} %param.27), channel_id=1, source_target_pairs={{0,28},{4,0},{8,4},{12,8},{16,12},{20,16},{24,20},{28,24},{1,29},{... | collective-permute-start | bytes 4616 | tf_op jit(solution)/shard_map/ppermute | solution.py:15
  4.1 10.8 %collective-permute-start.3 = (f32[3,128]{1,0:T(4,128)}, f32[3,128]{1,0:T(4,128)S(1)}, u32[]{:S(2)}, u32[]{:S(2)}) collective-permute-start(f32[3,128]{1,0:T(4,128)} %param.27), channel_id=1, source_target_pairs={{0,4},{4,8},{8,12},{12,16},{16,20},{20,24},{24,28},{28,0},{1,5},{5... | collective-permute-start | bytes 4616 | tf_op jit(solution)/shard_map/ppermute | solution.py:15
  4.1 19.9 %collective-permute-start.4 = (f32[16,128]{1,0:T(8,128)}, f32[16,128]{1,0:T(8,128)S(1)}, u32[]{:S(2)}, u32[]{:S(2)}) collective-permute-start(f32[16,128]{1,0:T(8,128)} %param.29), channel_id=1, source_target_pairs={{0,4},{4,8},{8,12},{12,16},{16,20},{20,24},{24,28},{28,0},{1,5},{5... | collective-permute-start | bytes 24584 | tf_op jit(solution)/shard_map/ppermute | solution.py:15
  6.0 2.2 %copy-start.7 = (f32[16,2]{0,1:T(2,128)S(1)}, f32[16,2]{0,1:T(2,128)}, u32[]{:S(2)}) copy-start(f32[16,2]{0,1:T(2,128)} %param.33) | copy-start | bytes 388
  6.0 2.4 %copy-start.2 = (f32[3,64,64]{2,1,0:T(8,128)S(1)}, f32[3,64,64]{2,1,0:T(8,128)}, u32[]{:S(2)}) copy-start(f32[3,64,64]{2,1,0:T(8,128)} %param.34) | copy-start | bytes 147460
  7.9 2.3 %copy-start.5 = (f32[8,16]{1,0:T(8,128)S(1)}, f32[8,16]{1,0:T(8,128)}, u32[]{:S(2)}) copy-start(f32[8,16]{1,0:T(8,128)} %param.31) | copy-start | bytes 1540
  11.0 23.1 %copy-start.1 = (f32[3,128]{1,0:T(4,128)S(1)}, f32[3,128]{1,0:T(4,128)}, u32[]{:S(2)}) copy-start(f32[3,128]{1,0:T(4,128)} %param.27) | copy-start | bytes 4612
  11.0 23.2 %copy-start.3 = (f32[3]{0:T(128)S(1)}, f32[3]{0:T(128)}, u32[]{:S(2)}) copy-start(f32[3]{0:T(128)} %constant.182.clone) | copy-start | bytes 40
  13.0 8.9 %collective-permute-start.6 = (f32[3,128]{1,0:T(4,128)S(1)}, f32[3,128]{1,0:T(4,128)S(1)}, u32[]{:S(2)}, u32[]{:S(2)}) collective-permute-start(f32[3,128]{1,0:T(4,128)S(1)} %collective-permute-done), channel_id=1, source_target_pairs={{0,28},{4,0},{8,4},{12,8},{16,12},{20,16},{24,20},{28,24},{1,29},{... | collective-permute-start | bytes 4616 | tf_op jit(solution)/shard_map/ppermute | solution.py:15
  14.9 8.6 %collective-permute-start.9 = (f32[3,128]{1,0:T(4,128)S(1)}, f32[3,128]{1,0:T(4,128)}, u32[]{:S(2)}, u32[]{:S(2)}) collective-permute-start(f32[3,128]{1,0:T(4,128)S(1)} %collective-permute-done.3), channel_id=1, source_target_pairs={{0,4},{4,8},{8,12},{12,16},{16,20},{20,24},{24,28},{28,0},{1,5},{5... | collective-permute-start | bytes 4616 | tf_op jit(solution)/shard_map/ppermute | solution.py:15
  16.8 3.9 %collective-permute-start.11 = (s32[128]{0:T(128)S(1)}, s32[128]{0:T(128)S(1)}, u32[]{:S(2)}, u32[]{:S(2)}) collective-permute-start(s32[128]{0:T(128)S(1)} %collective-permute-done.5), channel_id=1, source_target_pairs={{0,4},{4,8},{8,12},{12,16},{16,20},{20,24},{24,28},{28,0},{1,5},{5... | collective-permute-start | bytes 1544 | tf_op jit(solution)/shard_map/ppermute | solution.py:15
  17.6 3.3 %collective-permute-start.8 = (s32[128]{0:T(128)S(1)}, s32[128]{0:T(128)S(1)}, u32[]{:S(2)}, u32[]{:S(2)}) collective-permute-start(s32[128]{0:T(128)S(1)} %collective-permute-done.2), channel_id=1, source_target_pairs={{0,28},{4,0},{8,4},{12,8},{16,12},{20,16},{24,20},{28,24},{1,29},{... | collective-permute-start | bytes 1544 | tf_op jit(solution)/shard_map/ppermute | solution.py:15
  20.8 3.5 %collective-permute-start.1 = (f32[16,128]{1,0:T(8,128)S(1)}, f32[16,128]{1,0:T(8,128)S(1)}, u32[]{:S(2)}, u32[]{:S(2)}) collective-permute-start(f32[16,128]{1,0:T(8,128)S(1)} %copy-done.6), channel_id=1, source_target_pairs={{0,28},{4,0},{8,4},{12,8},{16,12},{20,16},{24,20},{28,24},{1,29},{... | collective-permute-start | bytes 24584 | tf_op jit(solution)/shard_map/ppermute | solution.py:15
  20.9 9.4 %collective-permute-start.17 = (s32[128]{0:T(128)S(1)}, s32[128]{0:T(128)S(1)}, u32[]{:S(2)}, u32[]{:S(2)}) collective-permute-start(s32[128]{0:T(128)S(1)} %collective-permute-done.11), channel_id=1, source_target_pairs={{0,4},{4,8},{8,12},{12,16},{16,20},{20,24},{24,28},{28,0},{1,5},{5... | collective-permute-start | bytes 1544 | tf_op jit(solution)/shard_map/ppermute | solution.py:15
  21.9 11.9 %collective-permute-start.14 = (s32[128]{0:T(128)S(1)}, s32[128]{0:T(128)S(1)}, u32[]{:S(2)}, u32[]{:S(2)}) collective-permute-start(s32[128]{0:T(128)S(1)} %collective-permute-done.8), channel_id=1, source_target_pairs={{0,28},{4,0},{8,4},{12,8},{16,12},{20,16},{24,20},{28,24},{1,29},{... | collective-permute-start | bytes 1544 | tf_op jit(solution)/shard_map/ppermute | solution.py:15
  23.5 10.6 %collective-permute-start.12 = (f32[3,128]{1,0:T(4,128)S(1)}, f32[3,128]{1,0:T(4,128)S(1)}, u32[]{:S(2)}, u32[]{:S(2)}) collective-permute-start(f32[3,128]{1,0:T(4,128)S(1)} %collective-permute-done.6), channel_id=1, source_target_pairs={{0,28},{4,0},{8,4},{12,8},{16,12},{20,16},{24,20},{28,24},{1,29},{... | collective-permute-start | bytes 4616 | tf_op jit(solution)/shard_map/ppermute | solution.py:15
  24.0 18.4 %collective-permute-start.15 = (f32[3,128]{1,0:T(4,128)}, f32[3,128]{1,0:T(4,128)S(1)}, u32[]{:S(2)}, u32[]{:S(2)}) collective-permute-start(f32[3,128]{1,0:T(4,128)} %collective-permute-done.9), channel_id=1, source_target_pairs={{0,4},{4,8},{8,12},{12,16},{16,20},{20,24},{24,28},{28,0},{1,5},{5... | collective-permute-start | bytes 4616 | tf_op jit(solution)/shard_map/ppermute | solution.py:15
  24.2 4.0 %collective-permute-start.10 = (f32[16,128]{1,0:T(8,128)S(1)}, f32[16,128]{1,0:T(8,128)S(1)}, u32[]{:S(2)}, u32[]{:S(2)}) collective-permute-start(f32[16,128]{1,0:T(8,128)S(1)} %collective-permute-done.4), channel_id=1, source_target_pairs={{0,4},{4,8},{8,12},{12,16},{16,20},{20,24},{24,28},{28,0},{1,5},{5... | collective-permute-start | bytes 24584 | tf_op jit(solution)/shard_map/ppermute | solution.py:15
  28.2 1.4 %collective-permute-start.7 = (f32[16,128]{1,0:T(8,128)S(1)}, f32[16,128]{1,0:T(8,128)S(1)}, u32[]{:S(2)}, u32[]{:S(2)}) collective-permute-start(f32[16,128]{1,0:T(8,128)S(1)} %collective-permute-done.1), channel_id=1, source_target_pairs={{0,28},{4,0},{8,4},{12,8},{16,12},{20,16},{24,20},{28,24},{1,29},{... | collective-permute-start | bytes 24584 | tf_op jit(solution)/shard_map/ppermute | solution.py:15
  29.6 4.0 %collective-permute-start.16 = (f32[16,128]{1,0:T(8,128)S(1)}, f32[16,128]{1,0:T(8,128)S(1)}, u32[]{:S(2)}, u32[]{:S(2)}) collective-permute-start(f32[16,128]{1,0:T(8,128)S(1)} %collective-permute-done.10), channel_id=1, source_target_pairs={{0,4},{4,8},{8,12},{12,16},{16,20},{20,24},{24,28},{28,0},{1,5},{5... | collective-permute-start | bytes 24584 | tf_op jit(solution)/shard_map/ppermute | solution.py:15
  30.3 3.5 %collective-permute-start.13 = (f32[16,128]{1,0:T(8,128)S(1)}, f32[16,128]{1,0:T(8,128)S(1)}, u32[]{:S(2)}, u32[]{:S(2)}) collective-permute-start(f32[16,128]{1,0:T(8,128)S(1)} %collective-permute-done.7), channel_id=1, source_target_pairs={{0,28},{4,0},{8,4},{12,8},{16,12},{20,16},{24,20},{28,24},{1,29},{... | collective-permute-start | bytes 24584 | tf_op jit(solution)/shard_map/ppermute | solution.py:15
  (3 other events, 4.8 us)
where the time goes:
time: 70.3 us; the launch traced here: 70 us
  starting transfers between devices  16.1 us (23%)
  other arithmetic  15.8 us (22%)
  blocking collectives  15.3 us (22%)
  waiting for transfers between devices  6.81 us (10%)
  matrix products  6.24 us (9%)
  between operations  4.81 us (7%)
  loops' own time  3.71 us (5%)
  local copies, waits for them, and re-layouts  1.22 us (2%)
    ppermute x18, starting transfers between devices, from_behind(): lax.ppermute(value, axis, [(i, (i + by) % size) for i in range(size)])  16.1 us
    all_gather x1, blocking collectives, shards(): lax.all_gather(features, 'chan', axis=0, tiled=True)  15.3 us
    mul x6, other arithmetic, table_of(): math.sqrt(2.0 / cut_radius)  10.8 us
    ppermute x18, waiting for transfers between devices, from_behind(): lax.ppermute(value, axis, [(i, (i + by) % size) for i in range(size)])  6.81 us
    another operation x6, loops' own time, contributions(): return lax.cond(active > 0, compute, skipped)  3.71 us
    dot_general x5, matrix products, compute(): jnp.einsum('ncb,nmab->cma', other_carried, pair_table, preferred_element_...  3.65 us
    reduce_sum x6, other arithmetic, table_of(): distance = jnp.sqrt(jnp.sum(separation * separation, axis=0) + soften)  2.27 us
  transfers between devices with their start and end apart: 18, of which 6 were waited for; matrix products, arithmetic and copies ran while one was open for 18% of the time, Pallas kernels for 0%

commit v1 on v0

--- a/solution.py
+++ b/solution.py
@@ -3,11 +3,33 @@
 import jax.numpy as jnp
 from jax import lax
 from jax.sharding import PartitionSpec as P
+from jax.lax import axis_index, axis_size, ppermute
 
 slab_width = 5.0 / 3.0
 cross_width = 48.0
 cut_radius = 5.0
 soften = 0.25
+
+
+def _name_wires(v0, in_dim):
+    v0 = jnp.moveaxis(v0, 0, in_dim)
+    latest = v0.shape
+    tmp = v0.reshape(*latest[:in_dim], latest[in_dim] * latest[in_dim + 1], *latest[in_dim + 2 :])
+    return tmp
+
+
+def save_ratios(field_in, mesh_dim, d0):
+    n = axis_size(mesh_dim)
+    views = tuple(((k, (k + 1) % n) for k in range(n)))
+    row_list = [field_in]
+    while len(row_list) < n:
+        val2 = ppermute(row_list[-1], mesh_dim, perm=views)
+        row_list.append(val2)
+    placed = axis_index(mesh_dim)
+    oldest = jnp.stack(row_list)
+    row_list = oldest[(placed - jnp.arange(n)) % n]
+    tile_out = _name_wires(row_list, d0)
+    return tile_out
 
 
 def from_behind(value, axis, by):
@@ -158,7 +180,7 @@
     mixed_tensor = jnp.einsum(
         "mpc,cma->pma",
         weights_out,
-        lax.all_gather(features, "chan", axis=0, tiled=True),
+        save_ratios(features, "chan", 0),
         precision=lax.Precision.HIGHEST,
     )
     return describe(mixed_tensor)

time: 70.3 us -> 73.9 us (1.051)
  waiting for transfers between devices: 6.81 us -> 23.1 us
  blocking collectives: 15.3 us -> 0 us
  starting transfers between devices: 16.1 us -> 18.3 us
    ppermute x0 -> x3, waiting for transfers between devices: none -> 17 us  [save_ratios(): val2 = ppermute(row_list[-1], mesh_dim, perm=views)]
    all_gather x1 -> x0, blocking collectives: 15.3 us -> none  [shards(): lax.all_gather(features, 'chan', axis=0, tiled=True)]
    ppermute x0 -> x3, starting transfers between devices: none -> 2.16 us  [save_ratios(): val2 = ppermute(row_list[-1], mesh_dim, perm=views)]
    ppermute x18, waiting for transfers between devices: 6.81 us -> 6 us  [from_behind(): lax.ppermute(value, axis, [(i, (i + by) % size) for i in range(size)])]
  transfers between devices with their start and end apart: 18 -> 21, of which waited for: 6 -> 7; matrix products, arithmetic and copies ran while one was open for 18% -> 17% of each run, Pallas kernels for 0% -> 0%
where the time goes in v1:
time: 73.9 us; the launch traced here: 73.6 us
  waiting for transfers between devices  23.1 us (31%)
  starting transfers between devices  18.3 us (25%)
  other arithmetic  15.8 us (21%)
  matrix products  6.25 us (8%)
  between operations  4.75 us (6%)
  loops' own time  3.69 us (5%)
  local copies, waits for them, and re-layouts  1.78 us (2%)
    ppermute x3, waiting for transfers between devices, save_ratios(): val2 = ppermute(row_list[-1], mesh_dim, perm=views)  17 us
    ppermute x18, starting transfers between devices, from_behind(): lax.ppermute(value, axis, [(i, (i + by) % size) for i in range(size)])  16.1 us
    mul x6, other arithmetic, table_of(): math.sqrt(2.0 / cut_radius)  10.8 us
    ppermute x18, waiting for transfers between devices, from_behind(): lax.ppermute(value, axis, [(i, (i + by) % size) for i in range(size)])  6 us
    another operation x6, loops' own time, contributions(): return lax.cond(active > 0, compute, skipped)  3.69 us
    dot_general x5, matrix products, compute(): jnp.einsum('ncb,nmab->cma', other_carried, pair_table, preferred_element_...  3.66 us
    reduce_sum x6, other arithmetic, table_of(): distance = jnp.sqrt(jnp.sum(separation * separation, axis=0) + soften)  2.23 us
    ppermute x3, starting transfers between devices, save_ratios(): val2 = ppermute(row_list[-1], mesh_dim, perm=views)  2.16 us
  transfers between devices with their start and end apart: 21, of which 7 were waited for; matrix products, arithmetic and copies ran while one was open for 17% of the time, Pallas kernels for 0%

profile of v1, /device:TPU:0, one launch (start us, length us, event | category | flops | bytes accessed | tf_op | source)
XLA Modules:
  0.0 73.6 jit_solution(138974212127674714)
XLA Ops:
  0.5 2.9 %collective-permute-start.2 = (s32[128]{0:T(128)}, s32[128]{0:T(128)S(1)}, u32[]{:S(2)}, u32[]{:S(2)}) collective-permute-start(s32[128]{0:T(128)} %param.28), channel_id=1, source_target_pairs={{0,28},{4,0},{8,4},{12,8},{16,12},{20,16},{24,20},{28,24},{1,29},{... | collective-permute-start | bytes 1544 | tf_op jit(solution)/shard_map/ppermute | solution.py:37
  4.9 0.9 %multiply_reduce_fusion.6 = (f32[128,128]{1,0:T(8,128)S(1)}, f32[3,128,128]{2,1,0:T(8,128)S(1)}) fusion(f32[3]{0:T(128)} %constant.244, f32[3]{0:T(128)} %constant.242.clone, f32[3,128]{1,0:T(4,128)} %param.27), kind=kLoop, calls=%fused_computation.333 | loop fusion | flops 376832 | bytes 263704 | tf_op jit(solution)/shard_map/reduce_sum | solution.py:44
  8.3 1.8 %divide_multiply_fusion.6 = f32[8,128,128]{2,1,0:T(8,128)S(1)} fusion(f32[128,128]{1,0:T(8,128)S(1)} %get-tuple-element.162, f32[128,128]{1,0:T(8,128)S(1)} %get-tuple-element.161, f32[8]{0:T(128)S(1)} %add_multiply_fusion.7), kind=kLoop, calls=%fused_computation.323 | loop fusion | flops 524288 | bytes 655392 | tf_op jit(solution)/shard_map/mul | solution.py:68
  11.6 1.9 %collective-permute-start.6 = (f32[3,128]{1,0:T(4,128)S(1)}, f32[3,128]{1,0:T(4,128)S(1)}, u32[]{:S(2)}, u32[]{:S(2)}) collective-permute-start(f32[3,128]{1,0:T(4,128)S(1)} %collective-permute-done), channel_id=1, source_target_pairs={{0,28},{4,0},{8,4},{12,8},{16,12},{20,16},{24,20},{28,24},{1,29},{... | collective-permute-start | bytes 4616 | tf_op jit(solution)/shard_map/ppermute | solution.py:37
  16.2 2.0 %collective-permute-start.8 = (s32[128]{0:T(128)S(1)}, s32[128]{0:T(128)S(1)}, u32[]{:S(2)}, u32[]{:S(2)}) collective-permute-start(s32[128]{0:T(128)S(1)} %collective-permute-done.2), channel_id=1, source_target_pairs={{0,28},{4,0},{8,4},{12,8},{16,12},{20,16},{24,20},{28,24},{1,29},{... | collective-permute-start | bytes 1544 | tf_op jit(solution)/shard_map/ppermute | solution.py:37
  20.5 2.1 %collective-permute-start.14 = (s32[128]{0:T(128)S(1)}, s32[128]{0:T(128)S(1)}, u32[]{:S(2)}, u32[]{:S(2)}) collective-permute-start(s32[128]{0:T(128)S(1)} %collective-permute-done.8), channel_id=1, source_target_pairs={{0,28},{4,0},{8,4},{12,8},{16,12},{20,16},{24,20},{28,24},{1,29},{... | collective-permute-start | bytes 1544 | tf_op jit(solution)/shard_map/ppermute | solution.py:37
  23.7 3.6 %collective-permute-done.10 = f32[16,128]{1,0:T(8,128)S(1)} collective-permute-done((f32[16,128]{1,0:T(8,128)S(1)}, f32[16,128]{1,0:T(8,128)S(1)}, u32[]{:S(2)}, u32[]{:S(2)}) %collective-permute-start.10) | collective-permute-done | bytes 8224 | tf_op jit(solution)/shard_map/ppermute | solution.py:37
  27.5 1.2 %collective-permute-done.7 = f32[16,128]{1,0:T(8,128)S(1)} collective-permute-done((f32[16,128]{1,0:T(8,128)S(1)}, f32[16,128]{1,0:T(8,128)S(1)}, u32[]{:S(2)}, u32[]{:S(2)}) %collective-permute-start.7) | collective-permute-done | bytes 8224 | tf_op jit(solution)/shard_map/ppermute | solution.py:37
  29.0 2.6 %collective-permute-start.13 = (f32[16,128]{1,0:T(8,128)S(1)}, f32[16,128]{1,0:T(8,128)S(1)}, u32[]{:S(2)}, u32[]{:S(2)}) collective-permute-start(f32[16,128]{1,0:T(8,128)S(1)} %collective-permute-done.7), channel_id=1, source_target_pairs={{0,28},{4,0},{8,4},{12,8},{16,12},{20,16},{24,20},{28,24},{1,29},{... | collective-permute-start | bytes 24584 | tf_op jit(solution)/shard_map/ppermute | solution.py:37
  31.6 1.1 %collective-permute-done.16 = f32[16,128]{1,0:T(8,128)S(1)} collective-permute-done((f32[16,128]{1,0:T(8,128)S(1)}, f32[16,128]{1,0:T(8,128)S(1)}, u32[]{:S(2)}, u32[]{:S(2)}) %collective-permute-start.16) | collective-permute-done | bytes 8224 | tf_op jit(solution)/shard_map/ppermute | solution.py:37
  33.3 3.7 %conditional.8 = (f32[16,9,128]{2,0,1:T(8,128)S(1)}) conditional(s32[]{:T(128)} %convert_element_type.108, () %tuple.45, (f32[3,128]{1,0:T(4,128)S(1)}, f32[3,128]{1,0:T(4,128)S(1)}, f32[3]{0:T(128)S(1)}, s32[]{:T(128)}, bf16[8,16,128]{2,1,0:T(8,128)(2,1)S(1)}) %tuple.113), branch_computations={%region_7.8_spmd, %region_8.10_spmd} | conditional | flops 41861136 | bytes 4435040 | solution.py:120
  34.5 1.8 %divide_multiply_fusion.2 = f32[8,128,128]{2,1,0:T(8,128)S(1)} fusion(f32[128,128]{1,0:T(8,128)S(1)} %get-tuple-element.143, f32[128,128]{1,0:T(8,128)S(1)} %get-tuple-element.142, f32[8]{0:T(128)S(1)} %add_multiply_fusion.2), kind=kLoop, calls=%fused_computation.106 | loop fusion | flops 524288 | bytes 655392 | tf_op jit(solution)/shard_map/cond/branch_1_fun/mul | solution.py:68
  37.0 4.4 %conditional.9 = (f32[16,9,128]{2,0,1:T(8,128)S(1)}) conditional(s32[]{:T(128)} %convert_element_type.110, () %tuple.47, (f32[3,128]{1,0:T(4,128)}, f32[3,128]{1,0:T(4,128)S(1)}, f32[3]{0:T(128)S(1)}, s32[]{:T(128)}, bf16[8,16,128]{2,1,0:T(8,128)(2,1)S(1)}) %tuple.114), branch_computations={%region_10.11_spmd, %region_11.13_spmd} | conditional | flops 41861136 | bytes 4435040 | solution.py:120
  38.9 1.8 %divide_multiply_fusion.3 = f32[8,128,128]{2,1,0:T(8,128)S(1)} fusion(f32[128,128]{1,0:T(8,128)S(1)} %get-tuple-element.147, f32[128,128]{1,0:T(8,128)S(1)} %get-tuple-element.146, f32[8]{0:T(128)S(1)} %add_multiply_fusion.3), kind=kLoop, calls=%fused_computation.156 | loop fusion | flops 524288 | bytes 655392 | tf_op jit(solution)/shard_map/cond/branch_1_fun/mul | solution.py:68
  41.4 3.7 %conditional.11 = (f32[16,9,128]{2,0,1:T(8,128)S(1)}) conditional(s32[]{:T(128)} %convert_element_type.114, () %tuple.51, (f32[3,128]{1,0:T(4,128)S(1)}, f32[3,128]{1,0:T(4,128)S(1)}, f32[3]{0:T(128)S(1)}, s32[]{:T(128)}, bf16[8,16,128]{2,1,0:T(8,128)(2,1)S(1)}) %tuple.115), branch_computations={%region_16.17_spmd, %region_17.19_spmd} | conditional | flops 41861136 | bytes 4435040 | solution.py:120
  42.6 1.8 %divide_multiply_fusion.5 = f32[8,128,128]{2,1,0:T(8,128)S(1)} fusion(f32[128,128]{1,0:T(8,128)S(1)} %get-tuple-element.155, f32[128,128]{1,0:T(8,128)S(1)} %get-tuple-element.154, f32[8]{0:T(128)S(1)} %add_multiply_fusion.5), kind=kLoop, calls=%fused_computation.256 | loop fusion | flops 524288 | bytes 655392 | tf_op jit(solution)/shard_map/cond/branch_1_fun/mul | solution.py:68
  45.1 3.7 %conditional.6 = (f32[16,9,128]{2,0,1:T(8,128)S(1)}) conditional(s32[]{:T(128)} %convert_element_type.104, () %tuple.41, (f32[3,128]{1,0:T(4,128)S(1)}, f32[3,128]{1,0:T(4,128)S(1)}, f32[3]{0:T(128)S(1)}, s32[]{:T(128)}, bf16[8,16,128]{2,1,0:T(8,128)(2,1)S(1)}) %tuple.116), branch_computations={%region_1.2_spmd, %region_2.4_spmd} | conditional | flops 41861136 | bytes 4435040 | solution.py:120
  46.3 1.8 %divide_multiply_fusion = f32[8,128,128]{2,1,0:T(8,128)S(1)} fusion(f32[128,128]{1,0:T(8,128)S(1)} %get-tuple-element.135, f32[128,128]{1,0:T(8,128)S(1)} %get-tuple-element.134, f32[8]{0:T(128)S(1)} %add_multiply_fusion), kind=kLoop, calls=%fused_computation.6 | loop fusion | flops 524288 | bytes 655392 | tf_op jit(solution)/shard_map/cond/branch_1_fun/mul | solution.py:68
  48.9 3.7 %conditional.7 = (f32[16,9,128]{2,0,1:T(8,128)S(1)}) conditional(s32[]{:T(128)} %convert_element_type.106, () %tuple.43, (f32[3,128]{1,0:T(4,128)S(1)}, f32[3,128]{1,0:T(4,128)S(1)}, f32[3]{0:T(128)S(1)}, s32[]{:T(128)}, bf16[8,16,128]{2,1,0:T(8,128)(2,1)S(1)}) %tuple.117), branch_computations={%region_4.5_spmd, %region_5.7_spmd} | conditional | flops 41861136 | bytes 4435040 | solution.py:120
  50.1 1.8 %divide_multiply_fusion.1 = f32[8,128,128]{2,1,0:T(8,128)S(1)} fusion(f32[128,128]{1,0:T(8,128)S(1)} %get-tuple-element.139, f32[128,128]{1,0:T(8,128)S(1)} %get-tuple-element.138, f32[8]{0:T(128)S(1)} %add_multiply_fusion.1), kind=kLoop, calls=%fused_computation.56 | loop fusion | flops 524288 | bytes 655392 | tf_op jit(solution)/shard_map/cond/branch_1_fun/mul | solution.py:68
  52.7 2.2 %collective-permute-start.18 = (f32[16,9,128]{2,0,1:T(8,128)S(1)}, f32[16,9,128]{2,0,1:T(8,128)S(1)}, u32[]{:S(2)}, u32[]{:S(2)}) collective-permute-start(f32[16,9,128]{2,0,1:T(8,128)S(1)} %add_multiply_fusion.6), channel_id=1, source_target_pairs={{0,1},{1,2},{2,3},{3,0},{4,5},{5,6},{6,7},{7,4},{8,9},{9,10},{10,1... | collective-permute-start | bytes 221192 | tf_op jit(solution)/shard_map/ppermute | solution.py:26
  54.8 4.5 %collective-permute-done.18 = f32[16,9,128]{2,0,1:T(8,128)S(1)} collective-permute-done((f32[16,9,128]{2,0,1:T(8,128)S(1)}, f32[16,9,128]{2,0,1:T(8,128)S(1)}, u32[]{:S(2)}, u32[]{:S(2)}) %collective-permute-start.18) | collective-permute-done | bytes 73760 | tf_op jit(solution)/shard_map/ppermute | solution.py:26
  59.4 6.4 %collective-permute-done.19 = f32[16,9,128]{2,0,1:T(8,128)S(1)} collective-permute-done((f32[16,9,128]{2,0,1:T(8,128)S(1)}, f32[16,9,128]{2,0,1:T(8,128)S(1)}, u32[]{:S(2)}, u32[]{:S(2)}) %collective-permute-start.19) | collective-permute-done | bytes 73760 | tf_op jit(solution)/shard_map/ppermute | solution.py:26
  65.8 6.1 %collective-permute-done.20 = f32[16,9,128]{2,0,1:T(8,128)S(1)} collective-permute-done((f32[16,9,128]{2,0,1:T(8,128)S(1)}, f32[16,9,128]{2,0,1:T(8,128)S(1)}, u32[]{:S(2)}, u32[]{:S(2)}) %collective-permute-start.20) | collective-permute-done | bytes 73760 | tf_op jit(solution)/shard_map/ppermute | solution.py:26
  (151 shorter events, 16.8 us)
Async XLA Ops:
  0.0 7.9 %copy-start = (f32[16,2]{0,1:T(2,128)S(1)}, f32[16,2]{0,1:T(2,128)}, u32[]{:S(2)}) copy-start(f32[16,2]{0,1:T(2,128)} %param.32) | copy-start | bytes 388
  0.0 15.4 %collective-permute-start.5 = (s32[128]{0:T(128)}, s32[128]{0:T(128)S(1)}, u32[]{:S(2)}, u32[]{:S(2)}) collective-permute-start(s32[128]{0:T(128)} %param.28), channel_id=1, source_target_pairs={{0,4},{4,8},{8,12},{12,16},{16,20},{20,24},{24,28},{28,0},{1,5},{5... | collective-permute-start | bytes 1544 | tf_op jit(solution)/shard_map/ppermute | solution.py:37
  0.5 15.7 %collective-permute-start.2 = (s32[128]{0:T(128)}, s32[128]{0:T(128)S(1)}, u32[]{:S(2)}, u32[]{:S(2)}) collective-permute-start(s32[128]{0:T(128)} %param.28), channel_id=1, source_target_pairs={{0,28},{4,0},{8,4},{12,8},{16,12},{20,16},{24,20},{28,24},{1,29},{... | collective-permute-start | bytes 1544 | tf_op jit(solution)/shard_map/ppermute | solution.py:37
  3.4 8.2 %collective-permute-start = (f32[3,128]{1,0:T(4,128)}, f32[3,128]{1,0:T(4,128)S(1)}, u32[]{:S(2)}, u32[]{:S(2)}) collective-permute-start(f32[3,128]{1,0:T(4,128)} %param.27), channel_id=1, source_target_pairs={{0,28},{4,0},{8,4},{12,8},{16,12},{20,16},{24,20},{28,24},{1,29},{... | collective-permute-start | bytes 4616 | tf_op jit(solution)/shard_map/ppermute | solution.py:37
  4.1 9.5 %collective-permute-start.3 = (f32[3,128]{1,0:T(4,128)}, f32[3,128]{1,0:T(4,128)S(1)}, u32[]{:S(2)}, u32[]{:S(2)}) collective-permute-start(f32[3,128]{1,0:T(4,128)} %param.27), channel_id=1, source_target_pairs={{0,4},{4,8},{8,12},{12,16},{16,20},{20,24},{24,28},{28,0},{1,5},{5... | collective-permute-start | bytes 4616 | tf_op jit(solution)/shard_map/ppermute | solution.py:37
  4.1 18.6 %collective-permute-start.4 = (f32[16,128]{1,0:T(8,128)}, f32[16,128]{1,0:T(8,128)S(1)}, u32[]{:S(2)}, u32[]{:S(2)}) collective-permute-start(f32[16,128]{1,0:T(8,128)} %param.29), channel_id=1, source_target_pairs={{0,4},{4,8},{8,12},{12,16},{16,20},{20,24},{24,28},{28,0},{1,5},{5... | collective-permute-start | bytes 24584 | tf_op jit(solution)/shard_map/ppermute | solution.py:37
  10.9 22.3 %copy-start.1 = (f32[3,128]{1,0:T(4,128)S(1)}, f32[3,128]{1,0:T(4,128)}, u32[]{:S(2)}) copy-start(f32[3,128]{1,0:T(4,128)} %param.27) | copy-start | bytes 4612
  10.9 22.3 %copy-start.3 = (f32[3]{0:T(128)S(1)}, f32[3]{0:T(128)}, u32[]{:S(2)}) copy-start(f32[3]{0:T(128)} %constant.242.clone) | copy-start | bytes 40
  11.6 8.9 %collective-permute-start.6 = (f32[3,128]{1,0:T(4,128)S(1)}, f32[3,128]{1,0:T(4,128)S(1)}, u32[]{:S(2)}, u32[]{:S(2)}) collective-permute-start(f32[3,128]{1,0:T(4,128)S(1)} %collective-permute-done), channel_id=1, source_target_pairs={{0,28},{4,0},{8,4},{12,8},{16,12},{20,16},{24,20},{28,24},{1,29},{... | collective-permute-start | bytes 4616 | tf_op jit(solution)/shard_map/ppermute | solution.py:37
  13.6 9.1 %collective-permute-start.9 = (f32[3,128]{1,0:T(4,128)S(1)}, f32[3,128]{1,0:T(4,128)}, u32[]{:S(2)}, u32[]{:S(2)}) collective-permute-start(f32[3,128]{1,0:T(4,128)S(1)} %collective-permute-done.3), channel_id=1, source_target_pairs={{0,4},{4,8},{8,12},{12,16},{16,20},{20,24},{24,28},{28,0},{1,5},{5... | collective-permute-start | bytes 4616 | tf_op jit(solution)/shard_map/ppermute | solution.py:37
  15.4 4.0 %collective-permute-start.11 = (s32[128]{0:T(128)S(1)}, s32[128]{0:T(128)S(1)}, u32[]{:S(2)}, u32[]{:S(2)}) collective-permute-start(s32[128]{0:T(128)S(1)} %collective-permute-done.5), channel_id=1, source_target_pairs={{0,4},{4,8},{8,12},{12,16},{16,20},{20,24},{24,28},{28,0},{1,5},{5... | collective-permute-start | bytes 1544 | tf_op jit(solution)/shard_map/ppermute | solution.py:37
  16.2 3.8 %collective-permute-start.8 = (s32[128]{0:T(128)S(1)}, s32[128]{0:T(128)S(1)}, u32[]{:S(2)}, u32[]{:S(2)}) collective-permute-start(s32[128]{0:T(128)S(1)} %collective-permute-done.2), channel_id=1, source_target_pairs={{0,28},{4,0},{8,4},{12,8},{16,12},{20,16},{24,20},{28,24},{1,29},{... | collective-permute-start | bytes 1544 | tf_op jit(solution)/shard_map/ppermute | solution.py:37
  19.5 3.8 %collective-permute-start.1 = (f32[16,128]{1,0:T(8,128)S(1)}, f32[16,128]{1,0:T(8,128)S(1)}, u32[]{:S(2)}, u32[]{:S(2)}) collective-permute-start(f32[16,128]{1,0:T(8,128)S(1)} %copy-done.6), channel_id=1, source_target_pairs={{0,28},{4,0},{8,4},{12,8},{16,12},{20,16},{24,20},{28,24},{1,29},{... | collective-permute-start | bytes 24584 | tf_op jit(solution)/shard_map/ppermute | solution.py:37
  20.0 9.0 %collective-permute-start.17 = (s32[128]{0:T(128)S(1)}, s32[128]{0:T(128)S(1)}, u32[]{:S(2)}, u32[]{:S(2)}) collective-permute-start(s32[128]{0:T(128)S(1)} %collective-permute-done.11), channel_id=1, source_target_pairs={{0,4},{4,8},{8,12},{12,16},{16,20},{20,24},{24,28},{28,0},{1,5},{5... | collective-permute-start | bytes 1544 | tf_op jit(solution)/shard_map/ppermute | solution.py:37
  20.5 12.4 %collective-permute-start.14 = (s32[128]{0:T(128)S(1)}, s32[128]{0:T(128)S(1)}, u32[]{:S(2)}, u32[]{:S(2)}) collective-permute-start(s32[128]{0:T(128)S(1)} %collective-permute-done.8), channel_id=1, source_target_pairs={{0,28},{4,0},{8,4},{12,8},{16,12},{20,16},{24,20},{28,24},{1,29},{... | collective-permute-start | bytes 1544 | tf_op jit(solution)/shard_map/ppermute | solution.py:37
  22.6 10.6 %collective-permute-start.12 = (f32[3,128]{1,0:T(4,128)S(1)}, f32[3,128]{1,0:T(4,128)S(1)}, u32[]{:S(2)}, u32[]{:S(2)}) collective-permute-start(f32[3,128]{1,0:T(4,128)S(1)} %collective-permute-done.6), channel_id=1, source_target_pairs={{0,28},{4,0},{8,4},{12,8},{16,12},{20,16},{24,20},{28,24},{1,29},{... | collective-permute-start | bytes 4616 | tf_op jit(solution)/shard_map/ppermute | solution.py:37
  22.7 18.7 %collective-permute-start.15 = (f32[3,128]{1,0:T(4,128)}, f32[3,128]{1,0:T(4,128)S(1)}, u32[]{:S(2)}, u32[]{:S(2)}) collective-permute-start(f32[3,128]{1,0:T(4,128)} %collective-permute-done.9), channel_id=1, source_target_pairs={{0,4},{4,8},{8,12},{12,16},{16,20},{20,24},{24,28},{28,0},{1,5},{5... | collective-permute-start | bytes 4616 | tf_op jit(solution)/shard_map/ppermute | solution.py:37
  23.3 4.0 %collective-permute-start.10 = (f32[16,128]{1,0:T(8,128)S(1)}, f32[16,128]{1,0:T(8,128)S(1)}, u32[]{:S(2)}, u32[]{:S(2)}) collective-permute-start(f32[16,128]{1,0:T(8,128)S(1)} %collective-permute-done.4), channel_id=1, source_target_pairs={{0,4},{4,8},{8,12},{12,16},{16,20},{20,24},{24,28},{28,0},{1,5},{5... | collective-permute-start | bytes 24584 | tf_op jit(solution)/shard_map/ppermute | solution.py:37
  27.3 1.4 %collective-permute-start.7 = (f32[16,128]{1,0:T(8,128)S(1)}, f32[16,128]{1,0:T(8,128)S(1)}, u32[]{:S(2)}, u32[]{:S(2)}) collective-permute-start(f32[16,128]{1,0:T(8,128)S(1)} %collective-permute-done.1), channel_id=1, source_target_pairs={{0,28},{4,0},{8,4},{12,8},{16,12},{20,16},{24,20},{28,24},{1,29},{... | collective-permute-start | bytes 24584 | tf_op jit(solution)/shard_map/ppermute | solution.py:37
  28.7 4.0 %collective-permute-start.16 = (f32[16,128]{1,0:T(8,128)S(1)}, f32[16,128]{1,0:T(8,128)S(1)}, u32[]{:S(2)}, u32[]{:S(2)}) collective-permute-start(f32[16,128]{1,0:T(8,128)S(1)} %collective-permute-done.10), channel_id=1, source_target_pairs={{0,4},{4,8},{8,12},{12,16},{16,20},{20,24},{24,28},{28,0},{1,5},{5... | collective-permute-start | bytes 24584 | tf_op jit(solution)/shard_map/ppermute | solution.py:37
  29.0 3.9 %collective-permute-start.13 = (f32[16,128]{1,0:T(8,128)S(1)}, f32[16,128]{1,0:T(8,128)S(1)}, u32[]{:S(2)}, u32[]{:S(2)}) collective-permute-start(f32[16,128]{1,0:T(8,128)S(1)} %collective-permute-done.7), channel_id=1, source_target_pairs={{0,28},{4,0},{8,4},{12,8},{16,12},{20,16},{24,20},{28,24},{1,29},{... | collective-permute-start | bytes 24584 | tf_op jit(solution)/shard_map/ppermute | solution.py:37
  52.7 6.7 %collective-permute-start.18 = (f32[16,9,128]{2,0,1:T(8,128)S(1)}, f32[16,9,128]{2,0,1:T(8,128)S(1)}, u32[]{:S(2)}, u32[]{:S(2)}) collective-permute-start(f32[16,9,128]{2,0,1:T(8,128)S(1)} %add_multiply_fusion.6), channel_id=1, source_target_pairs={{0,1},{1,2},{2,3},{3,0},{4,5},{5,6},{6,7},{7,4},{8,9},{9,10},{10,1... | collective-permute-start | bytes 221192 | tf_op jit(solution)/shard_map/ppermute | solution.py:26
  59.3 6.4 %collective-permute-start.19 = (f32[16,9,128]{2,0,1:T(8,128)S(1)}, f32[16,9,128]{2,0,1:T(8,128)S(1)}, u32[]{:S(2)}, u32[]{:S(2)}) collective-permute-start(f32[16,9,128]{2,0,1:T(8,128)S(1)} %collective-permute-done.18), channel_id=1, source_target_pairs={{0,1},{1,2},{2,3},{3,0},{4,5},{5,6},{6,7},{7,4},{8,9},{9,10},{10,1... | collective-permute-start | bytes 221192 | tf_op jit(solution)/shard_map/ppermute | solution.py:26
  65.8 6.2 %collective-permute-start.20 = (f32[16,9,128]{2,0,1:T(8,128)S(1)}, f32[16,9,128]{2,0,1:T(8,128)S(1)}, u32[]{:S(2)}, u32[]{:S(2)}) collective-permute-start(f32[16,9,128]{2,0,1:T(8,128)S(1)} %collective-permute-done.19), channel_id=1, source_target_pairs={{0,1},{1,2},{2,3},{3,0},{4,5},{5,6},{6,7},{7,4},{8,9},{9,10},{10,1... | collective-permute-start | bytes 221192 | tf_op jit(solution)/shard_map/ppermute | solution.py:26
  (6 other events, 13.1 us)
